TPU v7x, 1024 devices: a whole 4x4x32 slice. The times are simulated.
1024 devices in a mesh: ctx: 16 (over y, x), pipe: 64 (over z, core).
Axes of the slice: x: 4, y: 4, z: 32, core: 2. Of those that a mesh axis runs over, the one named last changes fastest.
Arguments:
- q_in: bfloat16 [64, 4096, 128], P('pipe', 'ctx'), may hold values from -6 to 6
- k_in: bfloat16 [64, 4096, 128], P('pipe', 'ctx'), may hold values from -6 to 6
- v_in: bfloat16 [64, 4096, 1024], P('pipe', 'ctx'), may hold values from -6 to 6
- gate_in: bfloat16 [64, 4096, 1024], P('pipe', 'ctx'), may hold values from -6 to 6
- out_grad: bfloat16 [64, 4096, 1024], P('pipe', 'ctx'), may hold values from -6 to 6
- conv_weight: bfloat16 [64, 3, 1024], P('pipe'), may hold values from -3.5 to 3.5
- bounds: int32 [64, 16], P('pipe'), may hold values from 0 to 256, as said below
Outputs:
- q_grad: bfloat16 [64, 4096, 128], P('pipe', 'ctx')
- k_grad: bfloat16 [64, 4096, 128], P('pipe', 'ctx')
- v_grad: bfloat16 [64, 4096, 1024], P('pipe', 'ctx')
- gate_grad: bfloat16 [64, 4096, 1024], P('pipe', 'ctx')
Inputs may be any that keep to these rules, and one draw needn't show every extreme that they name: bounds[s, c] is the offset within slice c of section s's sequence (of 256 tokens) at which a new document begins, or 256 where none begins at an offset of that slice; in slice 0 a document begins at offset 0 whatever bounds[s, 0] holds.
All inputs are finite; a program needn't handle non-finite values.
Results may differ from a plain program's by a relative error of at most 0.0015.
Values may be sent and summed in bfloat16 or wider, within the bound.
A program may use at most 128 MiB of HBM per device.

v0:
```python
import jax
import jax.numpy as jnp
from jax import lax
from jax.sharding import PartitionSpec as P

HEADS = 8
F = 16
DV = 128
CONV = 3
TOK_DEV = 256


half_root = 0.7071067811865476
highest = lax.Precision.HIGHEST


def from_behind(value, axis, steps):
    count = lax.axis_size(axis)
    pairs = [(source, (source + steps) % count) for source in range(count)]
    return lax.ppermute(value, axis, pairs)


def carried_in(part, axis, combine, identity, reverse):
    count = lax.axis_size(axis)
    place = lax.axis_index(axis)
    ahead = count - 1 - place if reverse else place
    gathered = jax.tree.map(lambda a: lax.all_gather(a, axis), part)
    state = jax.tree.map(lambda a, e: jnp.zeros_like(a) + jnp.asarray(e, a.dtype), part, identity)

    def one(hop, state):
        source = count - 1 - hop if reverse else hop
        return combine(
            state, jax.tree.map(lambda a: lax.dynamic_index_in_dim(a, source, 0, False), gathered)
        )

    return lax.fori_loop(0, ahead, one, state)


def expand_columns(inputs):
    heads, width, tokens = inputs.shape
    outer = (inputs[:, :, None, :] * inputs[:, None, :, :]).reshape(heads, width * width, tokens)
    ones_row = jnp.ones((heads, 1, tokens), jnp.float32)
    return jnp.concatenate([ones_row, inputs, outer * half_root], axis=1)


def columns_back(grads, inputs):
    heads, width, tokens = inputs.shape
    linear = grads[:, 1 : 1 + width]
    square = grads[:, 1 + width :].reshape(heads, width, width, tokens)
    both = jnp.sum(square * inputs[:, None, :, :], axis=2) + jnp.sum(
        square * inputs[:, :, None, :], axis=1
    )
    return linear + both * half_root


def segment_link(earlier, later):
    state_early, norm_early, reset_early, rows_early, valid_early = earlier
    state_late, norm_late, reset_late, rows_late, valid_late = later
    passing = 1.0 - reset_late
    return (
        state_late + passing * state_early,
        norm_late + passing * norm_early,
        jnp.maximum(reset_early, reset_late),
        rows_late + (1.0 - valid_late) * rows_early,
        jnp.maximum(valid_early, valid_late),
    )


def on_device(q_in, k_in, v_in, gate_in, out_grad, conv_weight, bounds):
    slice_index = lax.axis_index("ctx")
    boundary = lax.dynamic_slice_in_dim(bounds[0], slice_index, 1)[0]
    position = jnp.arange(TOK_DEV)
    before_doc = (position < boundary).astype(jnp.float32)
    opening = boundary % TOK_DEV
    after_doc = (position >= opening).astype(jnp.float32)
    in_newdoc = position >= boundary
    causal_mask = (position[:, None] >= position[None, :]) & (
        in_newdoc[:, None] == in_newdoc[None, :]
    )
    resets = (boundary < TOK_DEV).astype(jnp.float32)
    present = jnp.ones((), jnp.float32)
    qk_scale = F ** (-0.25)
    edge = CONV - 1
    incoming = from_behind(out_grad, "pipe", -1)[0].astype(jnp.float32)
    queries = (
        jnp.transpose(q_in[0].astype(jnp.float32).reshape(TOK_DEV, HEADS, F), (1, 2, 0)) * qk_scale
    )
    keys_scaled = (
        jnp.transpose(k_in[0].astype(jnp.float32).reshape(TOK_DEV, HEADS, F), (1, 2, 0)) * qk_scale
    )
    values = v_in[0].astype(jnp.float32).reshape(TOK_DEV, HEADS, DV)
    gate_rows = gate_in[0].astype(jnp.float32)
    conv_taps = conv_weight[0].astype(jnp.float32)
    query_phi = expand_columns(queries)
    key_phi = expand_columns(keys_scaled)
    key_used = key_phi * after_doc[None, None, :]
    local_state = jnp.einsum("het,thd->hed", key_used, values, precision=highest)
    local_norm = jnp.sum(key_used, axis=2)
    tail_rows = gate_rows[TOK_DEV - edge :] * after_doc[TOK_DEV - edge :, None]
    identity = (
        jnp.zeros_like(local_state),
        jnp.zeros_like(local_norm),
        jnp.zeros((), jnp.float32),
        jnp.zeros_like(tail_rows),
        jnp.zeros((), jnp.float32),
    )
    prefix = carried_in(
        (local_state, local_norm, resets, tail_rows, present), "ctx", segment_link, identity, False
    )
    state_in, norm_in, tail_prev = (prefix[0], prefix[1], prefix[3])
    affine = jnp.einsum("hft,hfs->hts", queries, keys_scaled, precision=highest)
    kernel = jnp.where(causal_mask[None], 1.0 + affine + 0.5 * affine * affine, 0.0)
    numerator = jnp.einsum("hts,shd->thd", kernel, values, precision=highest) + before_doc[
        :, None, None
    ] * jnp.einsum("het,hed->thd", query_phi, state_in, precision=highest)
    denominator = jnp.sum(kernel, axis=2).T + before_doc[:, None] * jnp.einsum(
        "het,he->th", query_phi, norm_in, precision=highest
    )
    attended = numerator / denominator[:, :, None]
    extended = jnp.concatenate([tail_prev, gate_rows], axis=0)
    mixed = jnp.zeros_like(gate_rows)
    for shift_by in range(CONV):
        source = position - shift_by
        usable = jnp.where(
            source >= 0, (source >= boundary) == in_newdoc, position < boundary
        ).astype(jnp.float32)
        mixed = (
            mixed
            + conv_taps[shift_by]
            * extended[edge - shift_by : edge - shift_by + TOK_DEV]
            * usable[:, None]
        )
    sigmoid_mix = jax.nn.sigmoid(mixed)
    grad_attended = (incoming * mixed * sigmoid_mix).reshape(TOK_DEV, HEADS, DV)
    grad_mixed = (
        incoming
        * attended.reshape(TOK_DEV, HEADS * DV)
        * sigmoid_mix
        * (1.0 + mixed * (1.0 - sigmoid_mix))
    )
    grad_numer = grad_attended / denominator[:, :, None]
    grad_denom = -jnp.sum(grad_attended * attended, axis=2) / denominator
    denom_cols = grad_denom.T
    query_used = query_phi * before_doc[None, None, :]
    back_state = jnp.einsum("het,thd->hed", query_used, grad_numer, precision=highest)
    back_norm = jnp.einsum("het,th->he", query_used, grad_denom, precision=highest)
    head_rows = grad_mixed[:edge] * before_doc[:edge, None]
    dot_terms = (
        jnp.einsum("thd,shd->hts", grad_numer, values, precision=highest) + denom_cols[:, :, None]
    )
    kernel_grad = jnp.where(causal_mask[None], dot_terms, 0.0) * (1.0 + affine)
    grad_qphi = before_doc[None, None, :] * (
        jnp.einsum("thd,hed->het", grad_numer, state_in, precision=highest)
        + norm_in[:, :, None] * denom_cols[:, None, :]
    )
    grad_queries = jnp.einsum(
        "hts,hfs->hft", kernel_grad, keys_scaled, precision=highest
    ) + columns_back(grad_qphi, queries)
    query_grad = (
        (jnp.transpose(grad_queries, (2, 0, 1)) * qk_scale)
        .reshape(1, TOK_DEV, HEADS * F)
        .astype(jnp.bfloat16)
    )
    suffix = carried_in(
        (back_state, back_norm, resets, head_rows, present), "ctx", segment_link, identity, True
    )
    suffix_state, suffix_norm, head_next = (suffix[0], suffix[1], suffix[3])
    grad_kphi = after_doc[None, None, :] * (
        jnp.einsum("shd,hed->hes", values, suffix_state, precision=highest)
        + suffix_norm[:, :, None]
    )
    grad_keys = jnp.einsum("hts,hft->hfs", kernel_grad, queries, precision=highest) + columns_back(
        grad_kphi, keys_scaled
    )
    grad_values = jnp.einsum("hts,thd->shd", kernel, grad_numer, precision=highest) + after_doc[
        :, None, None
    ] * jnp.einsum("hes,hed->shd", key_phi, suffix_state, precision=highest)
    ext_grad = jnp.concatenate([grad_mixed, head_next], axis=0)
    grad_gate = jnp.zeros_like(gate_rows)
    for shift_by in range(CONV):
        target = position + shift_by
        usable = jnp.where(
            target < TOK_DEV, (target >= boundary) == in_newdoc, position >= opening
        ).astype(jnp.float32)
        grad_gate = (
            grad_gate
            + conv_taps[shift_by] * ext_grad[shift_by : shift_by + TOK_DEV] * usable[:, None]
        )
    key_grad = (
        (jnp.transpose(grad_keys, (2, 0, 1)) * qk_scale)
        .reshape(1, TOK_DEV, HEADS * F)
        .astype(jnp.bfloat16)
    )
    value_grad = grad_values.reshape(1, TOK_DEV, HEADS * DV).astype(jnp.bfloat16)
    gate_grad = grad_gate.reshape(1, TOK_DEV, HEADS * DV).astype(jnp.bfloat16)
    delivered = from_behind((query_grad, key_grad, value_grad, gate_grad), "pipe", -1)
    result = (delivered[0], delivered[1], delivered[2], delivered[3])
    return result


def solution(mesh):
    in_specs = (
        P("pipe", "ctx", None),
        P("pipe", "ctx", None),
        P("pipe", "ctx", None),
        P("pipe", "ctx", None),
        P("pipe", "ctx", None),
        P("pipe", None, None),
        P("pipe", None),
    )
    out_specs = (
        P("pipe", "ctx", None),
        P("pipe", "ctx", None),
        P("pipe", "ctx", None),
        P("pipe", "ctx", None),
    )
    return jax.shard_map(
        on_device, mesh=mesh, in_specs=in_specs, out_specs=out_specs, check_vma=False
    )
```

profile of v0, /device:TPU:1, one launch (start us, length us, event | category | flops | bytes accessed | tf_op | source)
XLA Modules:
  0.0 602.2 jit_solution(781910256709084567)
XLA Ops:
  19.1 14.2 %collective-permute-start = (bf16[1,256,1024]{2,1,0:T(8,128)(2,1)}, bf16[1,256,1024]{2,1,0:T(8,128)(2,1)}, u32[]{:S(2)}, u32[]{:S(2)}) collective-permute-start(bf16[1,256,1024]{2,1,0:T(8,128)(2,1)} %param.15), channel_id=1, source_target_pairs={{0,63},{1,0},{2,1},{3,2},{4,3},{5,4},{6,5},{7,6},{8,7},{9,8},{10,9... | collective-permute-start | bytes 1572872 | tf_op jit(solution)/shard_map/ppermute | solution.py:20
  33.2 29.1 %all-reduce.2 = (f32[16]{0:T(128)}, f32[16]{0:T(128)}) all-reduce(f32[16]{0:T(128)S(1)} %dynamic-update-slice, f32[16]{0:T(128)S(1)} %dynamic-update-slice.1), channel_id=1, replica_groups=mesh['ctx'=16,'pipe'=64] {'ctx'}, use_global_device_ids=true, to_apply=%add | all-reduce | flops 32 | bytes 256
  64.4 20.1 %all-gather.6 = f32[16,2,1024]{2,1,0:T(2,128)} all-gather(f32[1,2,1024]{2,1,0:T(2,128)S(1)} %fusion.54), channel_id=4, replica_groups=mesh['ctx'=16,'pipe'=64] {'ctx'}, dimensions={0}, use_global_device_ids=true | all-gather | bytes 139264 | tf_op jit(solution)/shard_map/all_gather | solution.py:27
  85.2 18.0 %all-gather.1 = f32[128,273]{1,0:T(8,128)} all-gather(f32[8,273]{1,0:T(8,128)S(1)} %multiply_reduce_fusion), channel_id=3, replica_groups=mesh['ctx'=16,'pipe'=64] {'ctx'}, dimensions={0}, use_global_device_ids=true | all-gather | bytes 148512 | tf_op jit(solution)/shard_map/all_gather | solution.py:27
  108.0 2.8 fusion.43
  112.1 2.4 convolution_bitcast_fusion
  114.5 71.9 %all-gather.11.cloned.1.call-done = f32[128,273,128]{2,0,1:T(8,128)} async-done(((f32[8,273,128]{2,0,1:T(8,128)}), f32[128,273,128]{2,0,1:T(8,128)}) %all-gather.11.cloned.1.call-update) | async-done | bytes 17891344 | tf_op jit(solution)/shard_map/all_gather | solution.py:27
  186.8 3.3 fusion.50
  190.7 5.4 fusion.12
  196.1 2.5 copy.47
  198.6 4.3 fusion.36
  202.9 2.3 fusion.34
  205.3 2.5 copy.34
  207.8 4.4 fusion.4
  218.2 2.4 fusion.2
  221.2 14.4 %add_multiply_fusion.1 = f32[8,273,256]{2,1,0:T(8,128)S(1)} fusion(f32[8,273,128]{2,1,0:T(8,128)S(1)} %get-tuple-element.303, f32[8,256]{1,0:T(8,128)S(1)} %bitcast_divide_fusion, f32[8,273]{1,0:T(8,128)S(1)} %get-tuple-element.302, f32[256]{0:T(256)} %copy-done.22, f32[256,8,128]{0,2,1:T(8,128)S(1)} %bitcast.153, f32[256,8]{0,1:T(8,128)S(1)} %fusion.57), kind=kOutput, calls=%fused_computation.14 | convolution fusion | flops 860723200 | bytes 4429344 | tf_op jit(solution)/shard_map/thd,hed->het/dot_general | solution.py:153
  244.5 106.3 %all-gather.7 = f32[16,2,1024]{2,1,0:T(2,128)} all-gather(f32[1,2,1024]{2,1,0:T(2,128)S(1)} %fusion.52), channel_id=7, replica_groups=mesh['ctx'=16,'pipe'=64] {'ctx'}, dimensions={0}, use_global_device_ids=true | all-gather | bytes 139264 | tf_op jit(solution)/shard_map/all_gather | solution.py:27
  350.8 20.2 %all-gather.4 = f32[128,273]{1,0:T(8,128)} all-gather(f32[8,273]{1,0:T(8,128)S(1)} %bitcast.174), channel_id=6, replica_groups=mesh['ctx'=16,'pipe'=64] {'ctx'}, dimensions={0}, use_global_device_ids=true | all-gather | bytes 148512 | tf_op jit(solution)/shard_map/all_gather | solution.py:27
  371.0 91.6 %all-gather.13.cloned.1.call-done = f32[128,273,128]{2,0,1:T(8,128)} async-done(((f32[8,273,128]{2,0,1:T(8,128)}), f32[128,273,128]{2,0,1:T(8,128)}) %all-gather.13.cloned.1.call-update) | async-done | bytes 17891344 | tf_op jit(solution)/shard_map/all_gather | solution.py:27
  462.7 101.8 %while.39 = (s32[]{:T(128)}, f32[8,273,128]{2,1,0:T(8,128)S(1)}, f32[8,273]{1,0:T(8,128)S(1)}, f32[2,1024]{1,0:T(2,128)S(1)}, s32[]{:T(128)}, /*index=5*/f32[16,...) while((s32[]{:T(128)}, f32[8,273,128]{2,1,0:T(8,128)S(1)}, ...), condition=%wide.region_8.9_spmd, body=%wide.region_7.8_spmd.sunk | while | flops 567576 | bytes 5642091 | solution.py:36
  564.5 3.0 convolution_multiply_fusion
  567.6 2.6 fusion.13
  574.7 4.1 collective-permute-start.3
  585.3 3.9 collective-permute-done.2
  (226 shorter events, 134.5 us)
Async XLA Ops:
  7.2 179.3 %all-gather.11.cloned.1.call-start = ((), (), s32[]{:S(2)}) async-start(), calls=%async_computation | async-start | bytes 19009536 | tf_op jit(solution)/shard_map/all_gather | solution.py:27
  10.3 74.2 %copy-start.23 = (f32[256]{0:T(256)}, f32[256]{0:T(256)S(1)}, u32[]{:S(2)}) copy-start(f32[256]{0:T(256)S(1)} %fusion.59) | copy-start | bytes 3076
  12.5 98.3 %copy-start.9 = (bf16[32,8,8,128]{3,2,1,0:T(8,128)(2,1)}, bf16[32,8,8,128]{3,2,1,0:T(8,128)(2,1)S(1)}, u32[]{:S(2)}) copy-start(bf16[32,8,8,128]{3,2,1,0:T(8,128)(2,1)S(1)} %copy.67) | copy-start | bytes 1572868
  14.3 48.6 %copy-start.13 = (bf16[1,256,128]{2,1,0:T(8,128)(2,1)S(1)}, bf16[1,256,128]{2,1,0:T(8,128)(2,1)}, u32[]{:S(2)}) copy-start(bf16[1,256,128]{2,1,0:T(8,128)(2,1)} %param.11) | copy-start | bytes 196612
  14.4 48.7 %copy-start.12 = (bf16[1,256,1024]{2,1,0:T(8,128)(2,1)S(1)}, bf16[1,256,1024]{2,1,0:T(8,128)(2,1)}, u32[]{:S(2)}) copy-start(bf16[1,256,1024]{2,1,0:T(8,128)(2,1)} %param.14) | copy-start | bytes 1572868
  15.6 447.0 %all-gather.13.cloned.1.call-start = ((), (), s32[]{:S(2)}) async-start(), calls=%async_computation.1 | async-start | bytes 19009536 | tf_op jit(solution)/shard_map/all_gather | solution.py:27
  19.1 179.5 %collective-permute-start = (bf16[1,256,1024]{2,1,0:T(8,128)(2,1)}, bf16[1,256,1024]{2,1,0:T(8,128)(2,1)}, u32[]{:S(2)}, u32[]{:S(2)}) collective-permute-start(bf16[1,256,1024]{2,1,0:T(8,128)(2,1)} %param.15), channel_id=1, source_target_pairs={{0,63},{1,0},{2,1},{3,2},{4,3},{5,4},{6,5},{7,6},{8,7},{9,8},{10,9... | collective-permute-start | bytes 1572872 | tf_op jit(solution)/shard_map/ppermute | solution.py:20
  63.1 43.1 %copy-start.21 = (bf16[1,3,1024]{2,1,0:T(4,128)(2,1)S(1)}, bf16[1,3,1024]{2,1,0:T(4,128)(2,1)}, u32[]{:S(2)}) copy-start(bf16[1,3,1024]{2,1,0:T(4,128)(2,1)} %param.16) | copy-start | bytes 18436
  106.2 112.0 %copy-start.22 = (f32[256]{0:T(256)}, f32[256]{0:T(256)S(1)}, u32[]{:S(2)}) copy-start(f32[256]{0:T(256)S(1)} %get-tuple-element.387) | copy-start | bytes 3076
  106.3 4.5 copy-start.14
  112.1 74.4 %copy-start.28 = (f32[16]{0:T(128)S(1)}, f32[16]{0:T(128)}, u32[]{:S(2)}) copy-start(f32[16]{0:T(128)} %get-tuple-element.560) | copy-start | bytes 196
  112.1 74.4 %copy-start.29 = (f32[16]{0:T(128)S(1)}, f32[16]{0:T(128)}, u32[]{:S(2)}) copy-start(f32[16]{0:T(128)} %get-tuple-element.563) | copy-start | bytes 196
  186.8 3.9 copy-start.7
  213.9 4.3 copy-start.8
  238.9 4.8 copy-start.26
  242.1 343.2 %collective-permute-start.1 = (bf16[1,256,128]{2,1,0:T(8,128)(2,1)}, bf16[1,256,128]{2,1,0:T(8,128)(2,1)}, u32[]{:S(2)}, u32[]{:S(2)}) collective-permute-start(bf16[1,256,128]{2,1,0:T(8,128)(2,1)} %copy.43), channel_id=1, source_target_pairs={{0,63},{1,0},{2,1},{3,2},{4,3},{5,4},{6,5},{7,6},{8,7},{9,8},{10,9... | collective-permute-start | bytes 196616 | tf_op jit(solution)/shard_map/ppermute | solution.py:20
  462.7 101.8 %copy-start.24 = (f32[256]{0:T(256)S(1)}, f32[256]{0:T(256)}, u32[]{:S(2)}) copy-start(f32[256]{0:T(256)} %copy-done.23) | copy-start | bytes 3076
  567.6 3.6 copy-start.4
  567.6 3.6 copy-start.25
  570.2 8.6 %copy-start.11 = (bf16[32,8,8,128]{3,2,1,0:T(8,128)(2,1)S(1)}, bf16[32,8,8,128]{3,2,1,0:T(8,128)(2,1)}, u32[]{:S(2)}) copy-start(bf16[32,8,8,128]{3,2,1,0:T(8,128)(2,1)} %copy-done.9) | copy-start | bytes 1572868
  573.2 16.1 %collective-permute-start.4 = (bf16[1,256,1024]{2,1,0:T(8,128)(2,1)}, bf16[1,256,1024]{2,1,0:T(8,128)(2,1)}, u32[]{:S(2)}, u32[]{:S(2)}) collective-permute-start(bf16[1,256,1024]{2,1,0:T(8,128)(2,1)} %fusion.44), channel_id=1, source_target_pairs={{0,63},{1,0},{2,1},{3,2},{4,3},{5,4},{6,5},{7,6},{8,7},{9,8},{10,9... | collective-permute-start | bytes 1572872 | tf_op jit(solution)/shard_map/ppermute | solution.py:20
  574.7 14.6 %collective-permute-start.3 = (bf16[1,256,1024]{2,1,0:T(8,128)(2,1)}, bf16[1,256,1024]{2,1,0:T(8,128)(2,1)}, u32[]{:S(2)}, u32[]{:S(2)}) collective-permute-start(bf16[1,256,1024]{2,1,0:T(8,128)(2,1)} %copy.52), channel_id=1, source_target_pairs={{0,63},{1,0},{2,1},{3,2},{4,3},{5,4},{6,5},{7,6},{8,7},{9,8},{10,9... | collective-permute-start | bytes 1572872 | tf_op jit(solution)/shard_map/ppermute | solution.py:20
  581.3 13.8 %copy-start.1 = (s32[1,16]{1,0:T(1,128)S(1)}, s32[1,16]{1,0:T(1,128)}, u32[]{:S(2)}) copy-start(s32[1,16]{1,0:T(1,128)} %param.17) | copy-start | bytes 196
  583.8 5.5 collective-permute-start.2
  (16 other events, 31.3 us)
Sparse Core Ops, SparseCore 0:
  15.7 170.6 all-gather.10
  213.5 248.9 all-gather.12
where the time goes:
time: 613 us; the launch traced here: 602 us
  blocking collectives  194 us (32%)
  waiting for transfers between devices  168 us (27%)
  local copies, waits for them, and re-layouts  83 us (14%)
  other arithmetic  51.3 us (8%)
  matrix products  47.6 us (8%)
  starting transfers between devices  23 us (4%)
  loops' own time  18.9 us (3%)
  between operations  17.3 us (3%)
    all_gather x4, blocking collectives, carried_in(): gathered = jax.tree.map(lambda a: lax.all_gather(a, axis), part)  165 us
    all_gather x2, waiting for transfers between devices, carried_in(): gathered = jax.tree.map(lambda a: lax.all_gather(a, axis), part)  164 us
    dynamic_slice x45, local copies, waits for them, and re-layouts, one(): lax.dynamic_index_in_dim(a, source, 0, False)  56.2 us
    unnamed x1, blocking collectives  29.1 us
    ppermute x5, starting transfers between devices, from_behind(): return lax.ppermute(value, axis, pairs)  22.9 us
    another operation x2, loops' own time, carried_in(): return lax.fori_loop(0, ahead, one, state)  18.9 us
    unnamed x76, local copies, waits for them, and re-layouts  14.9 us
    dot_general x1, matrix products, on_device(): jnp.einsum('thd,hed->het', grad_numer, state_in, precision=highest)  14.4 us
  transfers between devices with their start and end apart: 7, of which 3 were waited for; matrix products, arithmetic and copies ran while one was open for 25% of the time, Pallas kernels for 0%

commit v1 on v0

v1 whole, which is shorter than its diff:
```python
import jax
import jax.numpy as jnp
from jax import lax
from jax.experimental import pallas as pl
from jax.experimental.pallas import tpu as pltpu
from jax.sharding import PartitionSpec as P

HEADS = 8
F = 16
DV = 128
T = 256
E = 160
N = 16
HALF = E // 2
WIDE = HEADS * DV
bf16 = jnp.bfloat16
f32 = jnp.float32
MESH = pl.DeviceIdType.MESH


def split(x):
    hi = x.astype(bf16)
    return hi, (x - hi.astype(f32)).astype(bf16)


def mm(a, b):
    return jnp.dot(a, b, preferred_element_type=f32)


def mm_nt(a, b):
    return lax.dot_general(a, b, (((1,), (1,)), ((), ())), preferred_element_type=f32)


def features(x, square):
    parts = [x, x * x * square]
    for r in range(1, 8):
        parts.append(x * pltpu.roll(x, r, axis=0))
    parts.append(x[:8] * x[8:])
    row = lax.broadcasted_iota(jnp.int32, (8, x.shape[1]), 0)
    parts.append(jnp.where(row == 0, 1.0, 0.0))
    return jnp.concatenate(parts, axis=0)


def features_back(g, x, square):
    out = g[:16] + g[16:32] * x * square
    for r in range(1, 8):
        gr = g[16 + 16 * r : 32 + 16 * r]
        out = out + gr * pltpu.roll(x, r, axis=0) + pltpu.roll(gr * x, 16 - r, axis=0)
    g8 = g[144:152]
    return out + jnp.concatenate([g8 * x[8:], g8 * x[:8]], axis=0)


def body(
    bounds, q_hbm, k_hbm, v_hbm, gate_hbm, og_hbm, w_hbm,
    dq_out, dk_out, dv_out, dgate_out,
    q_in, k_in, v_in, gate_in, w_in, cot, tail, head_next,
    q_t, k_t, phiq_hi, phiq_lo, phik_hi, phik_lo, qt_hi, qt_lo, kt_hi, kt_lo,
    mask, mask_t, u_all, numden, inv_all, ga_all, dsl, mixed_all,
    gn_hi, gn_lo, z_hi, z_lo, gmix, dv_acc, dq_t, dk_t,
    norm_own, norm_got, norm_in, norm_col, gd_rows, bnorm_own, bnorm_got, bnorm_col,
    s_own, s_got, pre_send, pre_got, b_own, b_got, suf_send, suf_got,
    dq_stage, dk_stage, dv_stage, dgate_stage,
    in_sem, cot_ss, cot_rs, halo_ss, halo_rs,
    n_ss, n_rs, bn_ss, bn_rs, p1_ss, p1_rs, p2_ss, p2_rs, p3_ss, p3_rs, p4_ss, p4_rs,
    out_ss, out_rs,
):
    me = lax.axis_index("ctx")
    pipe = lax.axis_index("pipe")
    pipes = lax.axis_size("pipe")
    before_pipe = {"pipe": lax.rem(pipe + pipes - 1, pipes)}
    after_pipe = {"pipe": lax.rem(pipe + 1, pipes)}

    barrier = pltpu.get_barrier_semaphore()
    for d in range(1, N):
        pl.semaphore_signal(barrier, inc=1, device_id={"ctx": lax.rem(me + d, N)}, device_id_type=MESH)
    pl.semaphore_signal(barrier, inc=1, device_id=before_pipe, device_id_type=MESH)
    pl.semaphore_signal(barrier, inc=1, device_id=after_pipe, device_id_type=MESH)

    loads = [
        pltpu.make_async_copy(src, dst, in_sem.at[i])
        for i, (src, dst) in enumerate(
            ((k_hbm, k_in), (q_hbm, q_in), (v_hbm, v_in), (gate_hbm, gate_in), (w_hbm, w_in))
        )
    ]
    for c in loads:
        c.start()

    def remote(src, dst, ss, rs, dev):
        return pltpu.make_async_remote_copy(
            src_ref=src, dst_ref=dst, send_sem=ss, recv_sem=rs, device_id=dev, device_id_type=MESH
        )

    def peer(d):
        return {"ctx": lax.rem(me + d, N)}

    b = bounds[0, me]
    opening = lax.rem(b, T)
    lane_t = lax.broadcasted_iota(jnp.int32, (1, T), 1)
    before_row = jnp.where(lane_t < b, 1.0, 0.0)
    after_row = jnp.where(lane_t >= opening, 1.0, 0.0)
    keep = [jnp.where(bounds[0, j] < T, 0.0, 1.0) for j in range(N)]
    head_lane = lax.shift_right_logical(lax.broadcasted_iota(jnp.int32, (1, 128), 1), 4)
    lane128 = lax.broadcasted_iota(jnp.int32, (1, 128), 1)
    row8 = lax.broadcasted_iota(jnp.int32, (8, 1), 0)

    def head16(h):
        return pl.ds(pl.multiple_of(h * 16, 16), 16)

    def head128(h):
        return pl.ds(pl.multiple_of(h * 128, 128), 128)

    loads[0].wait()
    k_t[...] = jnp.transpose(k_in[...].astype(f32)) * 0.5

    def key_features(h, norm):
        phi = features(k_t[head16(h), :], 1.0) * after_row
        hi, lo = split(phi)
        phik_hi[h] = hi
        phik_lo[h] = lo
        row = jnp.broadcast_to(jnp.where(row8 == h, 1.0, 0.0), (8, T)).astype(bf16)
        return norm + mm_nt(row, hi) + mm_nt(row, lo)

    norm = lax.fori_loop(0, HEADS, key_features, jnp.zeros((8, E), f32))
    norm_own[...] = jnp.concatenate([norm, jnp.zeros((8, T - E), f32)], axis=1)

    pl.semaphore_wait(barrier, N + 1)
    sends = []

    def start(c):
        c.start()
        sends.append(c)

    def gather_start(own, got, ss, rs):
        for d in range(1, N):
            start(remote(own, got.at[me], ss.at[d], rs.at[d], peer(d)))
        got[me] = own[...]

    def gather_wait(own, got, ss, rs):
        for d in range(1, N):
            remote(own, got.at[lax.rem(me + N - d, N)], ss.at[d], rs.at[d], peer(d)).wait_recv()

    gather_start(norm_own, norm_got, n_ss, n_rs)
    start(remote(gate_hbm.at[pl.ds(T - 16, 16)], tail, halo_ss.at[0], halo_rs.at[0], peer(1)))
    cots = []
    for i in range(4):
        cols = pl.ds(i * 256, 256)
        c = remote(og_hbm.at[:, cols], cot.at[:, cols], cot_ss.at[i], cot_rs.at[i], before_pipe)
        start(c)
        cots.append(c)

    loads[2].wait()

    def local_state(h, carry):
        v = v_in[:, head128(h)]
        s = mm(phik_hi[h], v) + mm(phik_lo[h], v)
        s_own[2 * h] = s[:HALF]
        s_own[2 * h + 1] = s[HALF:]
        return carry

    lax.fori_loop(0, HEADS, local_state, 0)

    def spread_start(own, got, ss, rs):
        for d in range(1, N):
            to = lax.rem(me + d, N)
            start(remote(own.at[to], got.at[me], ss.at[d], rs.at[d], {"ctx": to}))
        got[me] = own[me]

    def spread_wait(own, got, ss, rs):
        for d in range(1, N):
            src = lax.rem(me + N - d, N)
            remote(own.at[src], got.at[src], ss.at[d], rs.at[d], {"ctx": src}).wait_recv()

    spread_start(s_own, s_got, p1_ss, p1_rs)

    loads[1].wait()
    q_t[...] = jnp.transpose(q_in[...].astype(f32)) * 0.5
    ti = lax.broadcasted_iota(jnp.int32, (T, T), 0)
    si = lax.broadcasted_iota(jnp.int32, (T, T), 1)
    t_new = jnp.where(ti >= b, 1, 0)
    s_new = jnp.where(si >= b, 1, 0)
    mask[...] = jnp.where((ti >= si) & (t_new == s_new), 1.0, 0.0)
    mask_t[...] = jnp.where((si >= ti) & (t_new == s_new), 1.0, 0.0)

    def query_head(h):
        return (jnp.where(head_lane == h, q_in[...].astype(f32), 0.0) * 0.25).astype(bf16)

    def value_and_one(h):
        return jnp.concatenate([v_in[:, head128(h)], jnp.ones((T, 128), bf16)], axis=1)

    def inside(h, carry):
        phi = features(q_t[head16(h), :], 0.5) * before_row
        hi, lo = split(phi)
        phiq_hi[h] = hi
        phiq_lo[h] = lo
        hi, lo = split(jnp.transpose(phi))
        qt_hi[h] = hi
        qt_lo[h] = lo
        u = 1.0 + mm_nt(query_head(h), k_in[...])
        u_all[h] = u
        hi, lo = split(mask[...] * (0.5 * u * u + 0.5))
        va = value_and_one(h)
        numden[h] = mm(hi, va) + mm(lo, va)
        return carry

    lax.fori_loop(0, HEADS, inside, 0)

    loads[3].wait()
    loads[4].wait()
    remote(gate_hbm.at[pl.ds(T - 16, 16)], tail, halo_ss.at[0], halo_rs.at[0], peer(1)).wait_recv()
    pos = lax.broadcasted_iota(jnp.int32, (T, 1), 0)
    row_new = jnp.where(pos >= b, 1, 0)
    prev = lax.rem(me + N - 1, N)
    prev_open = lax.rem(bounds[0, prev], T)
    has_prev = jnp.where(me > 0, 1.0, 0.0)
    tail254 = jnp.where(prev_open <= T - 2, has_prev, 0.0)

    def usable(j):
        same = jnp.where(jnp.where(pos - j >= b, 1, 0) == row_new, 1.0, 0.0)
        return jnp.where(pos - j >= 0, same, jnp.where(pos < b, 1.0, 0.0))

    use1, use2 = usable(1), usable(2)

    def conv(h, carry):
        cols = head128(h)
        g = gate_in[:, cols].astype(f32)
        last = tail[:, cols].astype(f32)
        r254 = last[14:15] * tail254
        r255 = last[15:16] * has_prev
        g1 = jnp.where(pos == 0, r255, pltpu.roll(g, 1, axis=0))
        g2 = jnp.where(pos == 0, r254, jnp.where(pos == 1, r255, pltpu.roll(g, 2, axis=0)))
        w = w_in[:, cols].astype(f32)
        mixed_all[:, cols] = w[0:1] * g + w[1:2] * (g1 * use1) + w[2:3] * (g2 * use2)
        return carry

    lax.fori_loop(0, HEADS, conv, 0)

    gather_wait(norm_own, norm_got, n_ss, n_rs)
    acc = jnp.zeros((8, T), f32)
    for j in range(N):
        acc = jnp.where(j < me, norm_got[j] + keep[j] * acc, acc)
    norm_in[...] = acc
    norm_col[...] = jnp.transpose(jnp.concatenate([acc, jnp.zeros((120, T), f32)], axis=0))
    for c in cots:
        c.wait_recv()

    def numer_grad(h, carry):
        cols = head128(h)
        n_hi, n_lo = split(jnp.broadcast_to(norm_in[pl.ds(h, 1), :E], (128, E)))
        den = (
            numden[h, :, 128:]
            + mm_nt(qt_hi[h], n_hi) + mm_nt(qt_hi[h], n_lo) + mm_nt(qt_lo[h], n_hi)
        )
        inv = 1.0 / den
        inv_all[h] = inv
        mixed = mixed_all[:, cols]
        sig = 1.0 / (1.0 + jnp.exp(-mixed))
        cs = cot[:, cols].astype(f32) * sig
        ga = cs * mixed
        ga_all[:, cols] = ga
        dsl[:, cols] = cs * (1.0 + mixed * (1.0 - sig))
        hi, lo = split(ga * inv)
        gn_hi[h] = hi
        gn_lo[h] = lo
        s = mm(phiq_hi[h], hi) + mm(phiq_hi[h], lo) + mm(phiq_lo[h], hi)
        b_own[2 * h] = s[:HALF]
        b_own[2 * h + 1] = s[HALF:]
        return carry

    lax.fori_loop(0, HEADS, numer_grad, 0)
    spread_start(b_own, b_got, p3_ss, p3_rs)

    spread_wait(s_own, s_got, p1_ss, p1_rs)
    acc = jnp.zeros((HALF, 128), f32)
    for j in range(N):
        pre_send[j] = acc
        if j < N - 1:
            acc = s_got[j] + keep[j] * acc
    spread_start(pre_send, pre_got, p2_ss, p2_rs)

    def value_grad(h, carry):
        ut = 1.0 + mm_nt(k_in[...], query_head(h))
        hi, lo = split(mask_t[...] * (0.5 * ut * ut + 0.5))
        dv_acc[:, head128(h)] = mm(hi, gn_hi[h]) + mm(hi, gn_lo[h]) + mm(lo, gn_hi[h])
        hi, lo = split(jnp.transpose(phik_hi[h].astype(f32) + phik_lo[h].astype(f32)))
        kt_hi[h] = hi
        kt_lo[h] = lo
        return carry

    lax.fori_loop(0, HEADS, value_grad, 0)

    spread_wait(b_own, b_got, p3_ss, p3_rs)
    acc = jnp.zeros((HALF, 128), f32)
    for j in reversed(range(N)):
        suf_send[j] = acc
        if j > 0:
            acc = b_got[j] + keep[j] * acc
    spread_start(suf_send, suf_got, p4_ss, p4_rs)

    spread_wait(pre_send, pre_got, p2_ss, p2_rs)

    def attended(h, bnorm):
        cols = head128(h)
        p_hi, p_lo = split(jnp.concatenate([pre_got[2 * h], pre_got[2 * h + 1]], axis=0))
        num = (
            numden[h, :, :128]
            + mm(qt_hi[h], p_hi) + mm(qt_hi[h], p_lo) + mm(qt_lo[h], p_hi)
        )
        inv = inv_all[h]
        y = num * inv
        gmix[:, cols] = dsl[:, cols] * y
        hi, lo = split(-(ga_all[:, cols] * inv * y))
        z_hi[h] = hi
        z_lo[h] = lo
        row = jnp.broadcast_to(jnp.where(row8 == h, 1.0, 0.0), (8, 128)).astype(bf16)
        gd = mm_nt(row, hi) + mm_nt(row, lo)
        gd_rows[h] = jnp.broadcast_to(jnp.sum(gd, axis=0, keepdims=True), (8, T))
        hi, lo = split(gd)
        return bnorm + mm_nt(hi, phiq_hi[h]) + mm_nt(hi, phiq_lo[h]) + mm_nt(lo, phiq_hi[h])

    bnorm = lax.fori_loop(0, HEADS, attended, jnp.zeros((8, E), f32))
    bnorm_own[...] = jnp.concatenate([bnorm, jnp.zeros((8, T - E), f32)], axis=1)
    gather_start(bnorm_own, bnorm_got, bn_ss, bn_rs)
    start(remote(gmix.at[pl.ds(0, 8)], head_next, halo_ss.at[1], halo_rs.at[1], peer(N - 1)))

    def scores_grad(h, carry):
        va = value_and_one(h)
        g_hi = jnp.concatenate([gn_hi[h], z_hi[h]], axis=1)
        g_lo = jnp.concatenate([gn_lo[h], z_lo[h]], axis=1)
        hi, lo = split((mm_nt(g_hi, va) + mm_nt(g_lo, va)) * (u_all[h] * mask[...]))
        qh = q_t[head16(h), :]
        kh = k_t[head16(h), :].astype(bf16)
        dk_t[head16(h), :] = mm(qh.astype(bf16), hi) + mm(qh.astype(bf16), lo)
        p_hi, p_lo = split(jnp.concatenate([pre_got[2 * h], pre_got[2 * h + 1]], axis=0))
        col = jnp.sum(jnp.where(lane128 == h, norm_col[:E], 0.0), axis=1, keepdims=True)
        g = (
            mm_nt(p_hi, gn_hi[h]) + mm_nt(p_hi, gn_lo[h]) + mm_nt(p_lo, gn_hi[h])
            + col * gd_rows[h, 0:1]
        )
        dq_t[head16(h), :] = (
            mm_nt(kh, hi) + mm_nt(kh, lo) + before_row * features_back(g, qh, 1.0)
        )
        return carry

    lax.fori_loop(0, HEADS, scores_grad, 0)
    dq_stage[...] = (jnp.transpose(dq_t[...]) * 0.5).astype(bf16)
    outs = [remote(dq_stage, dq_out, out_ss.at[0], out_rs.at[0], before_pipe)]
    start(outs[0])

    remote(gmix.at[pl.ds(0, 8)], head_next, halo_ss.at[1], halo_rs.at[1], peer(N - 1)).wait_recv()
    nxt = lax.rem(me + 1, N)
    b_next = bounds[0, nxt]
    has_next = jnp.where(me < N - 1, 1.0, 0.0)
    next0 = jnp.where(b_next > 0, has_next, 0.0)
    next1 = jnp.where(b_next > 1, has_next, 0.0)

    def usable_back(j):
        same = jnp.where(jnp.where(pos + j >= b, 1, 0) == row_new, 1.0, 0.0)
        return jnp.where(pos + j < T, same, jnp.where(pos >= opening, 1.0, 0.0))

    back1, back2 = usable_back(1), usable_back(2)

    def conv_back(h, carry):
        cols = head128(h)
        g = gmix[:, cols]
        nr = head_next[:, cols]
        r0 = nr[0:1] * next0
        r1 = nr[1:2] * next1
        g1 = jnp.where(pos == T - 1, r0, pltpu.roll(g, T - 1, axis=0))
        g2 = jnp.where(pos == T - 1, r1, jnp.where(pos == T - 2, r0, pltpu.roll(g, T - 2, axis=0)))
        w = w_in[:, cols].astype(f32)
        out = w[0:1] * g + w[1:2] * (g1 * back1) + w[2:3] * (g2 * back2)
        dgate_stage[:, cols] = out.astype(bf16)
        return carry

    lax.fori_loop(0, HEADS, conv_back, 0)
    outs.append(remote(dgate_stage, dgate_out, out_ss.at[1], out_rs.at[1], before_pipe))
    start(outs[1])

    gather_wait(bnorm_own, bnorm_got, bn_ss, bn_rs)
    acc = jnp.zeros((8, T), f32)
    for j in reversed(range(N)):
        acc = jnp.where(j > me, bnorm_got[j] + keep[j] * acc, acc)
    bnorm_col[...] = jnp.transpose(jnp.concatenate([acc, jnp.zeros((120, T), f32)], axis=0))
    spread_wait(suf_send, suf_got, p4_ss, p4_rs)

    def key_value_grad(h, carry):
        cols = head128(h)
        s_hi, s_lo = split(jnp.concatenate([suf_got[2 * h], suf_got[2 * h + 1]], axis=0))
        dv = (
            dv_acc[:, cols]
            + mm(kt_hi[h], s_hi) + mm(kt_hi[h], s_lo) + mm(kt_lo[h], s_hi)
        )
        dv_stage[:, cols] = dv.astype(bf16)
        v = v_in[:, cols]
        col = jnp.sum(jnp.where(lane128 == h, bnorm_col[:E], 0.0), axis=1, keepdims=True)
        g = mm_nt(s_hi, v) + mm_nt(s_lo, v) + col
        dk_t[head16(h), :] += after_row * features_back(g, k_t[head16(h), :], 2.0)
        return carry

    for i in range(4):
        lax.fori_loop(2 * i, 2 * i + 2, key_value_grad, 0)
        cols = pl.ds(i * 256, 256)
        outs.append(remote(dv_stage.at[:, cols], dv_out.at[:, cols], out_ss.at[3 + i], out_rs.at[3 + i], before_pipe))
        start(outs[-1])
    dk_stage[...] = (jnp.transpose(dk_t[...]) * 0.5).astype(bf16)
    outs.append(remote(dk_stage, dk_out, out_ss.at[2], out_rs.at[2], before_pipe))
    start(outs[-1])

    for c in sends:
        c.wait_send()
    for c in outs:
        c.wait_recv()


def on_device(q_in, k_in, v_in, gate_in, out_grad, conv_weight, bounds):
    def vm(shape, dtype=f32):
        return pltpu.VMEM(shape, dtype)

    def sems(n):
        return pltpu.SemaphoreType.DMA((n,))

    any_spec = pl.BlockSpec(memory_space=pl.ANY)
    big = (N, HALF, 128)
    heads = (HEADS, T, 128)
    scratch = [
        vm((T, 128), bf16), vm((T, 128), bf16), vm((T, WIDE), bf16), vm((T, WIDE), bf16),
        vm((3, WIDE), bf16), vm((T, WIDE), bf16), vm((16, WIDE), bf16), vm((8, WIDE)),
        vm((128, T)), vm((128, T)),
        *[vm((HEADS, E, T), bf16)] * 4,
        *[vm((HEADS, T, E), bf16)] * 4,
        vm((T, T)), vm((T, T)), vm((HEADS, T, T)), vm((HEADS, T, 256)), vm(heads),
        vm((T, WIDE)), vm((T, WIDE)), vm((T, WIDE)),
        vm(heads, bf16), vm(heads, bf16), vm(heads, bf16), vm(heads, bf16),
        vm((T, WIDE)), vm((T, WIDE)), vm((128, T)), vm((128, T)),
        vm((8, T)), vm((N, 8, T)), vm((8, T)), vm((T, 128)), vm((HEADS, 8, T)),
        vm((8, T)), vm((N, 8, T)), vm((T, 128)),
        *[vm(big)] * 8,
        vm((T, 128), bf16), vm((T, 128), bf16), vm((T, WIDE), bf16), vm((T, WIDE), bf16),
        sems(5), sems(4), sems(4), sems(2), sems(2),
        *[sems(N)] * 12,
        sems(7), sems(7),
    ]
    narrow = jax.ShapeDtypeStruct((T, HEADS * F), bf16)
    wide = jax.ShapeDtypeStruct((T, WIDE), bf16)
    dq, dk, dv, dgate = pl.pallas_call(
        body,
        out_shape=(narrow, narrow, wide, wide),
        in_specs=[pl.BlockSpec(memory_space=pltpu.SMEM)] + [any_spec] * 6,
        out_specs=(any_spec,) * 4,
        scratch_shapes=scratch,
        compiler_params=pltpu.CompilerParams(
            collective_id=0, has_side_effects=True, vmem_limit_bytes=60 * 1024 * 1024
        ),
        name="section_backward",
    )(bounds, q_in[0], k_in[0], v_in[0], gate_in[0], out_grad[0], conv_weight[0])
    return dq[None], dk[None], dv[None], dgate[None]


def solution(mesh):
    tokens = P("pipe", "ctx", None)
    return jax.shard_map(
        on_device,
        mesh=mesh,
        in_specs=(tokens,) * 5 + (P("pipe", None, None), P("pipe", None)),
        out_specs=(tokens,) * 4,
        check_vma=False,
    )
```

time: 613 us -> 78.7 us (0.13)
  the two profiles are of different devices: /device:TPU:1 before, /device:TPU:6 now
where the time goes in v1:
time: 78.7 us; the launch traced here: 78.2 us
  Pallas kernels  72.7 us (92%)
  local copies, waits for them, and re-layouts  4.86 us (6%)
    pallas_call x1, Pallas kernels, on_device(): pl.pallas_call(body, out_shape=(narrow, narrow, wide, wide), in_specs=[pl...  72.7 us
    unnamed x8, local copies, waits for them, and re-layouts  4.86 us

profile of v1, /device:TPU:6, one launch (start us, length us, event | category | flops | bytes accessed | tf_op | source)
XLA Modules:
  0.0 78.2 jit_solution(7679310408045828506)
XLA Ops:
  0.6 72.7 %section_backward.1 = (bf16[256,128]{1,0:T(8,128)(2,1)}, bf16[256,128]{1,0:T(8,128)(2,1)}, bf16[256,1024]{1,0:T(8,128)(2,1)}, bf16[256,1024]{1,0:T(8,128)(2,1)}) custom-call(s32[1,16]{1,0:T(1,128)} %bounds.1, bf16[256,128]{1,0:T(8,128)(2,1)} %bitcast.15, bf16[256,128]{1,0:T(8,128)(2,1)} %bitcast.16, bf16[256,1024]{1,0:T(8,128)(2,1)} %bitcast.10, ...), custom_call_target="tpu_custom_call" | custom-call | tf_op jit(solution)/shard_map/section_backward/pallas_call | solution.py:445
  73.3 0.0 copy-start.1
  73.3 1.5 %copy.15 = bf16[1,256,128]{2,1,0:T(8,128)(2,1)} copy(bf16[1,256,128]{2,1,0:T(8,128)(2,1)} %bitcast.18) | data formatting | bytes 131072
  74.8 0.0 copy-done.1
  74.8 0.6 copy.16
  75.4 0.0 copy-start
  75.4 1.9 %copy.17 = bf16[1,256,1024]{2,1,0:T(8,128)(2,1)} copy(bf16[1,256,1024]{2,1,0:T(8,128)(2,1)} %bitcast.14) | data formatting | bytes 1048576
  77.4 0.0 copy-done
  77.4 0.8 %copy.18 = bf16[1,256,1024]{2,1,0:T(8,128)(2,1)} copy(bf16[1,256,1024]{2,1,0:T(8,128)(2,1)S(1)} %bitcast.13) | data formatting | bytes 1048576
Async XLA Ops:
  73.3 1.5 %copy-start.1 = (bf16[256,128]{1,0:T(8,128)(2,1)S(1)}, bf16[256,128]{1,0:T(8,128)(2,1)}, u32[]{:S(2)}) copy-start(bf16[256,128]{1,0:T(8,128)(2,1)} %get-tuple-element.9) | copy-start | bytes 196612
  75.4 1.9 %copy-start = (bf16[256,1024]{1,0:T(8,128)(2,1)S(1)}, bf16[256,1024]{1,0:T(8,128)(2,1)}, u32[]{:S(2)}) copy-start(bf16[256,1024]{1,0:T(8,128)(2,1)} %get-tuple-element.11) | copy-start | bytes 1572868

commit v2 on v1

--- a/solution.py
+++ b/solution.py
@@ -55,8 +55,8 @@
     dq_out, dk_out, dv_out, dgate_out,
     q_in, k_in, v_in, gate_in, w_in, cot, tail, head_next,
     q_t, k_t, phiq_hi, phiq_lo, phik_hi, phik_lo, qt_hi, qt_lo, kt_hi, kt_lo,
-    mask, mask_t, u_all, numden, inv_all, ga_all, dsl, mixed_all,
-    gn_hi, gn_lo, z_hi, z_lo, gmix, dv_acc, dq_t, dk_t,
+    mask, mask_t, u_all, numden, inv_all, ga_all, dsl, silu,
+    gn_hi, gn_lo, mu_hi, mu_lo, ku_t, gmix, dv_acc, dq_t, dk_t,
     norm_own, norm_got, norm_in, norm_col, gd_rows, bnorm_own, bnorm_got, bnorm_col,
     s_own, s_got, pre_send, pre_got, b_own, b_got, suf_send, suf_got,
     dq_stage, dk_stage, dv_stage, dgate_stage,
@@ -103,6 +103,19 @@
     lane128 = lax.broadcasted_iota(jnp.int32, (1, 128), 1)
     row8 = lax.broadcasted_iota(jnp.int32, (8, 1), 0)
 
+    def by_groups(fn, carry, before=None, after=None, size=4):
+        def group(g, carry):
+            index = [g * size + r for r in range(size)]
+            for i in index if before else ():
+                before(i)
+            for i in index:
+                carry = fn(i, carry)
+            for i in index if after else ():
+                after(i)
+            return carry
+
+        return lax.fori_loop(0, HEADS // size, group, carry)
+
     def head16(h):
         return pl.ds(pl.multiple_of(h * 16, 16), 16)
 
@@ -120,7 +133,7 @@
         row = jnp.broadcast_to(jnp.where(row8 == h, 1.0, 0.0), (8, T)).astype(bf16)
         return norm + mm_nt(row, hi) + mm_nt(row, lo)
 
-    norm = lax.fori_loop(0, HEADS, key_features, jnp.zeros((8, E), f32))
+    norm = by_groups(key_features, jnp.zeros((8, E), f32))
     norm_own[...] = jnp.concatenate([norm, jnp.zeros((8, T - E), f32)], axis=1)
 
     pl.semaphore_wait(barrier, N + 1)
@@ -141,36 +154,57 @@
 
     gather_start(norm_own, norm_got, n_ss, n_rs)
     start(remote(gate_hbm.at[pl.ds(T - 16, 16)], tail, halo_ss.at[0], halo_rs.at[0], peer(1)))
-    cots = []
-    for i in range(4):
-        cols = pl.ds(i * 256, 256)
-        c = remote(og_hbm.at[:, cols], cot.at[:, cols], cot_ss.at[i], cot_rs.at[i], before_pipe)
-        start(c)
-        cots.append(c)
+
+    def cot_piece(i):
+        cols = head128(lax.rem(i + lax.shift_right_logical(me, 1), HEADS))
+        return remote(og_hbm.at[:, cols], cot.at[:, cols], cot_ss.at[i], cot_rs.at[i], before_pipe)
+
+    for i in range(HEADS):
+        start(cot_piece(i))
 
     loads[2].wait()
 
-    def local_state(h, carry):
+    def chunk_start(own, got, ss, rs, j):
+        @pl.when(j != me)
+        def _():
+            remote(own.at[j], got.at[me], ss.at[j], rs.at[me], {"ctx": j}).start()
+
+        @pl.when(j == me)
+        def _():
+            got[me] = own[me]
+
+    def spread_start(own, got, ss, rs):
+        for d in range(1, N):
+            to = lax.rem(me + d, N)
+            remote(own.at[to], got.at[me], ss.at[to], rs.at[me], {"ctx": to}).start()
+        got[me] = own[me]
+
+    def spread_wait(own, got, ss, rs):
+        for d in range(1, N):
+            src = lax.rem(me + N - d, N)
+            remote(own.at[src], got.at[src], ss.at[src], rs.at[src], {"ctx": src}).wait_recv()
+
+    def spread_sent(own, got, ss, rs):
+        for d in range(1, N):
+            to = lax.rem(me + d, N)
+            remote(own.at[to], got.at[me], ss.at[to], rs.at[me], {"ctx": to}).wait_send()
+
+    def turn(i):
+        return lax.rem(i + lax.shift_right_logical(me, 1), HEADS)
+
+    def local_state(i, carry):
+        h = turn(i)
         v = v_in[:, head128(h)]
         s = mm(phik_hi[h], v) + mm(phik_lo[h], v)
         s_own[2 * h] = s[:HALF]
         s_own[2 * h + 1] = s[HALF:]
         return carry
 
-    lax.fori_loop(0, HEADS, local_state, 0)
-
-    def spread_start(own, got, ss, rs):
-        for d in range(1, N):
-            to = lax.rem(me + d, N)
-            start(remote(own.at[to], got.at[me], ss.at[d], rs.at[d], {"ctx": to}))
-        got[me] = own[me]
-
-    def spread_wait(own, got, ss, rs):
-        for d in range(1, N):
-            src = lax.rem(me + N - d, N)
-            remote(own.at[src], got.at[src], ss.at[d], rs.at[d], {"ctx": src}).wait_recv()
-
-    spread_start(s_own, s_got, p1_ss, p1_rs)
+    def state_sends(i):
+        chunk_start(s_own, s_got, p1_ss, p1_rs, 2 * turn(i))
+        chunk_start(s_own, s_got, p1_ss, p1_rs, 2 * turn(i) + 1)
+
+    by_groups(local_state, 0, after=state_sends)
 
     loads[1].wait()
     q_t[...] = jnp.transpose(q_in[...].astype(f32)) * 0.5
@@ -202,7 +236,7 @@
         numden[h] = mm(hi, va) + mm(lo, va)
         return carry
 
-    lax.fori_loop(0, HEADS, inside, 0)
+    by_groups(inside, 0)
 
     loads[3].wait()
     loads[4].wait()
@@ -229,10 +263,13 @@
         g1 = jnp.where(pos == 0, r255, pltpu.roll(g, 1, axis=0))
         g2 = jnp.where(pos == 0, r254, jnp.where(pos == 1, r255, pltpu.roll(g, 2, axis=0)))
         w = w_in[:, cols].astype(f32)
-        mixed_all[:, cols] = w[0:1] * g + w[1:2] * (g1 * use1) + w[2:3] * (g2 * use2)
-        return carry
-
-    lax.fori_loop(0, HEADS, conv, 0)
+        mixed = w[0:1] * g + w[1:2] * (g1 * use1) + w[2:3] * (g2 * use2)
+        sig = 1.0 / (1.0 + jnp.exp(-mixed))
+        silu[:, cols] = mixed * sig
+        dsl[:, cols] = sig * (1.0 + mixed * (1.0 - sig))
+        return carry
+
+    by_groups(conv, 0)
 
     gather_wait(norm_own, norm_got, n_ss, n_rs)
     acc = jnp.zeros((8, T), f32)
@@ -240,10 +277,9 @@
         acc = jnp.where(j < me, norm_got[j] + keep[j] * acc, acc)
     norm_in[...] = acc
     norm_col[...] = jnp.transpose(jnp.concatenate([acc, jnp.zeros((120, T), f32)], axis=0))
-    for c in cots:
-        c.wait_recv()
-
-    def numer_grad(h, carry):
+
+    def numer_grad(i, carry):
+        h = turn(i)
         cols = head128(h)
         n_hi, n_lo = split(jnp.broadcast_to(norm_in[pl.ds(h, 1), :E], (128, E)))
         den = (
@@ -252,12 +288,8 @@
         )
         inv = 1.0 / den
         inv_all[h] = inv
-        mixed = mixed_all[:, cols]
-        sig = 1.0 / (1.0 + jnp.exp(-mixed))
-        cs = cot[:, cols].astype(f32) * sig
-        ga = cs * mixed
+        ga = cot[:, cols].astype(f32) * silu[:, cols]
         ga_all[:, cols] = ga
-        dsl[:, cols] = cs * (1.0 + mixed * (1.0 - sig))
         hi, lo = split(ga * inv)
         gn_hi[h] = hi
         gn_lo[h] = lo
@@ -266,8 +298,11 @@
         b_own[2 * h + 1] = s[HALF:]
         return carry
 
-    lax.fori_loop(0, HEADS, numer_grad, 0)
-    spread_start(b_own, b_got, p3_ss, p3_rs)
+    def grad_sends(i):
+        chunk_start(b_own, b_got, p3_ss, p3_rs, 2 * turn(i))
+        chunk_start(b_own, b_got, p3_ss, p3_rs, 2 * turn(i) + 1)
+
+    by_groups(numer_grad, 0, before=lambda i: cot_piece(i).wait_recv(), after=grad_sends)
 
     spread_wait(s_own, s_got, p1_ss, p1_rs)
     acc = jnp.zeros((HALF, 128), f32)
@@ -284,9 +319,20 @@
         hi, lo = split(jnp.transpose(phik_hi[h].astype(f32) + phik_lo[h].astype(f32)))
         kt_hi[h] = hi
         kt_lo[h] = lo
-        return carry
-
-    lax.fori_loop(0, HEADS, value_grad, 0)
+        v = v_in[:, head128(h)]
+        mu = u_all[h] * mask[...]
+        hi, lo = split((mm_nt(gn_hi[h], v) + mm_nt(gn_lo[h], v)) * mu)
+        qh = q_t[head16(h), :].astype(bf16)
+        kh = k_t[head16(h), :].astype(bf16)
+        dk_t[head16(h), :] = mm(qh, hi) + mm(qh, lo)
+        dq_t[head16(h), :] = mm_nt(kh, hi) + mm_nt(kh, lo)
+        hi, lo = split(mu)
+        mu_hi[h] = hi
+        mu_lo[h] = lo
+        ku_t[head16(h), :] = mm_nt(kh, hi) + mm_nt(kh, lo)
+        return carry
+
+    by_groups(value_grad, 0)
 
     spread_wait(b_own, b_got, p3_ss, p3_rs)
     acc = jnp.zeros((HALF, 128), f32)
@@ -307,44 +353,18 @@
         )
         inv = inv_all[h]
         y = num * inv
-        gmix[:, cols] = dsl[:, cols] * y
+        gmix[:, cols] = cot[:, cols].astype(f32) * dsl[:, cols] * y
         hi, lo = split(-(ga_all[:, cols] * inv * y))
-        z_hi[h] = hi
-        z_lo[h] = lo
         row = jnp.broadcast_to(jnp.where(row8 == h, 1.0, 0.0), (8, 128)).astype(bf16)
         gd = mm_nt(row, hi) + mm_nt(row, lo)
         gd_rows[h] = jnp.broadcast_to(jnp.sum(gd, axis=0, keepdims=True), (8, T))
         hi, lo = split(gd)
         return bnorm + mm_nt(hi, phiq_hi[h]) + mm_nt(hi, phiq_lo[h]) + mm_nt(lo, phiq_hi[h])
 
-    bnorm = lax.fori_loop(0, HEADS, attended, jnp.zeros((8, E), f32))
+    bnorm = by_groups(attended, jnp.zeros((8, E), f32))
     bnorm_own[...] = jnp.concatenate([bnorm, jnp.zeros((8, T - E), f32)], axis=1)
     gather_start(bnorm_own, bnorm_got, bn_ss, bn_rs)
     start(remote(gmix.at[pl.ds(0, 8)], head_next, halo_ss.at[1], halo_rs.at[1], peer(N - 1)))
-
-    def scores_grad(h, carry):
-        va = value_and_one(h)
-        g_hi = jnp.concatenate([gn_hi[h], z_hi[h]], axis=1)
-        g_lo = jnp.concatenate([gn_lo[h], z_lo[h]], axis=1)
-        hi, lo = split((mm_nt(g_hi, va) + mm_nt(g_lo, va)) * (u_all[h] * mask[...]))
-        qh = q_t[head16(h), :]
-        kh = k_t[head16(h), :].astype(bf16)
-        dk_t[head16(h), :] = mm(qh.astype(bf16), hi) + mm(qh.astype(bf16), lo)
-        p_hi, p_lo = split(jnp.concatenate([pre_got[2 * h], pre_got[2 * h + 1]], axis=0))
-        col = jnp.sum(jnp.where(lane128 == h, norm_col[:E], 0.0), axis=1, keepdims=True)
-        g = (
-            mm_nt(p_hi, gn_hi[h]) + mm_nt(p_hi, gn_lo[h]) + mm_nt(p_lo, gn_hi[h])
-            + col * gd_rows[h, 0:1]
-        )
-        dq_t[head16(h), :] = (
-            mm_nt(kh, hi) + mm_nt(kh, lo) + before_row * features_back(g, qh, 1.0)
-        )
-        return carry
-
-    lax.fori_loop(0, HEADS, scores_grad, 0)
-    dq_stage[...] = (jnp.transpose(dq_t[...]) * 0.5).astype(bf16)
-    outs = [remote(dq_stage, dq_out, out_ss.at[0], out_rs.at[0], before_pipe)]
-    start(outs[0])
 
     remote(gmix.at[pl.ds(0, 8)], head_next, halo_ss.at[1], halo_rs.at[1], peer(N - 1)).wait_recv()
     nxt = lax.rem(me + 1, N)
@@ -372,9 +392,25 @@
         dgate_stage[:, cols] = out.astype(bf16)
         return carry
 
-    lax.fori_loop(0, HEADS, conv_back, 0)
-    outs.append(remote(dgate_stage, dgate_out, out_ss.at[1], out_rs.at[1], before_pipe))
-    start(outs[1])
+    by_groups(conv_back, 0)
+    dgate_copy = remote(dgate_stage, dgate_out, out_ss.at[9], out_rs.at[9], before_pipe)
+    start(dgate_copy)
+
+    def scores_grad(h, carry):
+        qh = q_t[head16(h), :]
+        gd = gd_rows[h, 0:1]
+        hi, lo = split(qh * gd)
+        dk_t[head16(h), :] += mm(hi, mu_hi[h]) + mm(hi, mu_lo[h]) + mm(lo, mu_hi[h])
+        p_hi, p_lo = split(jnp.concatenate([pre_got[2 * h], pre_got[2 * h + 1]], axis=0))
+        col = jnp.sum(jnp.where(lane128 == h, norm_col[:E], 0.0), axis=1, keepdims=True)
+        g = mm_nt(p_hi, gn_hi[h]) + mm_nt(p_hi, gn_lo[h]) + mm_nt(p_lo, gn_hi[h]) + col * gd
+        dq_t[head16(h), :] += ku_t[head16(h), :] * gd + before_row * features_back(g, qh, 1.0)
+        return carry
+
+    by_groups(scores_grad, 0)
+    dq_stage[...] = (jnp.transpose(dq_t[...]) * 0.5).astype(bf16)
+    dq_copy = remote(dq_stage, dq_out, out_ss.at[8], out_rs.at[8], before_pipe)
+    start(dq_copy)
 
     gather_wait(bnorm_own, bnorm_got, bn_ss, bn_rs)
     acc = jnp.zeros((8, T), f32)
@@ -382,6 +418,10 @@
         acc = jnp.where(j > me, bnorm_got[j] + keep[j] * acc, acc)
     bnorm_col[...] = jnp.transpose(jnp.concatenate([acc, jnp.zeros((120, T), f32)], axis=0))
     spread_wait(suf_send, suf_got, p4_ss, p4_rs)
+
+    def dv_copy(h):
+        cols = head128(h)
+        return remote(dv_stage.at[:, cols], dv_out.at[:, cols], out_ss.at[h], out_rs.at[h], before_pipe)
 
     def key_value_grad(h, carry):
         cols = head128(h)
@@ -397,18 +437,20 @@
         dk_t[head16(h), :] += after_row * features_back(g, k_t[head16(h), :], 2.0)
         return carry
 
-    for i in range(4):
-        lax.fori_loop(2 * i, 2 * i + 2, key_value_grad, 0)
-        cols = pl.ds(i * 256, 256)
-        outs.append(remote(dv_stage.at[:, cols], dv_out.at[:, cols], out_ss.at[3 + i], out_rs.at[3 + i], before_pipe))
-        start(outs[-1])
+    by_groups(key_value_grad, 0, after=lambda i: dv_copy(i).start())
     dk_stage[...] = (jnp.transpose(dk_t[...]) * 0.5).astype(bf16)
-    outs.append(remote(dk_stage, dk_out, out_ss.at[2], out_rs.at[2], before_pipe))
-    start(outs[-1])
+    dk_copy = remote(dk_stage, dk_out, out_ss.at[10], out_rs.at[10], before_pipe)
+    start(dk_copy)
 
     for c in sends:
         c.wait_send()
-    for c in outs:
+    spread_sent(s_own, s_got, p1_ss, p1_rs)
+    spread_sent(pre_send, pre_got, p2_ss, p2_rs)
+    spread_sent(b_own, b_got, p3_ss, p3_rs)
+    spread_sent(suf_send, suf_got, p4_ss, p4_rs)
+    for h in range(HEADS):
+        dv_copy(h).wait_send()
+    for c in [dq_copy, dgate_copy, dk_copy] + [dv_copy(h) for h in range(HEADS)]:
         c.wait_recv()
 
 
@@ -430,30 +472,31 @@
         *[vm((HEADS, T, E), bf16)] * 4,
         vm((T, T)), vm((T, T)), vm((HEADS, T, T)), vm((HEADS, T, 256)), vm(heads),
         vm((T, WIDE)), vm((T, WIDE)), vm((T, WIDE)),
-        vm(heads, bf16), vm(heads, bf16), vm(heads, bf16), vm(heads, bf16),
+        vm(heads, bf16), vm(heads, bf16), vm((HEADS, T, T), bf16), vm((HEADS, T, T), bf16), vm((128, T)),
         vm((T, WIDE)), vm((T, WIDE)), vm((128, T)), vm((128, T)),
         vm((8, T)), vm((N, 8, T)), vm((8, T)), vm((T, 128)), vm((HEADS, 8, T)),
         vm((8, T)), vm((N, 8, T)), vm((T, 128)),
         *[vm(big)] * 8,
         vm((T, 128), bf16), vm((T, 128), bf16), vm((T, WIDE), bf16), vm((T, WIDE), bf16),
-        sems(5), sems(4), sems(4), sems(2), sems(2),
+        sems(5), sems(HEADS), sems(HEADS), sems(2), sems(2),
         *[sems(N)] * 12,
-        sems(7), sems(7),
+        sems(11), sems(11),
     ]
-    narrow = jax.ShapeDtypeStruct((T, HEADS * F), bf16)
-    wide = jax.ShapeDtypeStruct((T, WIDE), bf16)
-    dq, dk, dv, dgate = pl.pallas_call(
+    narrow = (T, HEADS * F)
+    wide = (T, WIDE)
+    shapes = (narrow, narrow, wide, wide)
+    results = pl.pallas_call(
         body,
-        out_shape=(narrow, narrow, wide, wide),
+        out_shape=tuple(pltpu.VMEM(x, bf16) for x in shapes),
         in_specs=[pl.BlockSpec(memory_space=pltpu.SMEM)] + [any_spec] * 6,
-        out_specs=(any_spec,) * 4,
+        out_specs=(pl.BlockSpec(memory_space=pltpu.VMEM),) * 4,
         scratch_shapes=scratch,
         compiler_params=pltpu.CompilerParams(
-            collective_id=0, has_side_effects=True, vmem_limit_bytes=60 * 1024 * 1024
+            collective_id=0, has_side_effects=True, vmem_limit_bytes=56 * 1024 * 1024
         ),
         name="section_backward",
     )(bounds, q_in[0], k_in[0], v_in[0], gate_in[0], out_grad[0], conv_weight[0])
-    return dq[None], dk[None], dv[None], dgate[None]
+    return tuple(x[None] for x in results)
 
 
 def solution(mesh):

time: 78.7 us -> 73.4 us (0.933)
  Pallas kernels: 72.7 us -> 69.8 us
  local copies, waits for them, and re-layouts: 4.86 us -> 2.85 us
    pallas_call x1, Pallas kernels: 72.7 us -> 69.8 us  [on_device(): pl.pallas_call(body, out_shape=tuple((pltpu.VMEM(x, bf16) for x in shapes...]
    unnamed x8 -> x4, local copies, waits for them, and re-layouts: 4.86 us -> 2.85 us
where the time goes in v2:
time: 73.4 us; the launch traced here: 73.2 us
  Pallas kernels  69.8 us (95%)
  local copies, waits for them, and re-layouts  2.85 us (4%)
    pallas_call x1, Pallas kernels, on_device(): pl.pallas_call(body, out_shape=tuple((pltpu.VMEM(x, bf16) for x in shapes...  69.8 us
    unnamed x4, local copies, waits for them, and re-layouts  2.85 us

profile of v2, /device:TPU:6, one launch (start us, length us, event | category | flops | bytes accessed | tf_op | source)
XLA Modules:
  0.0 73.2 jit_solution(622184679352220551)
XLA Ops:
  0.6 69.8 %section_backward.1 = (bf16[256,128]{1,0:T(8,128)(2,1)S(1)}, bf16[256,128]{1,0:T(8,128)(2,1)S(1)}, bf16[256,1024]{1,0:T(8,128)(2,1)S(1)}, bf16[256,1024]{1,0:T(8,128)(2,1)S(1)}) custom-call(s32[1,16]{1,0:T(1,128)} %bounds.1, bf16[256,128]{1,0:T(8,128)(2,1)} %bitcast.17, bf16[256,128]{1,0:T(8,128)(2,1)} %bitcast.18, bf16[256,1024]{1,0:T(8,128)(2,1)} %bitcast.14, ...), custom_call_target="tpu_custom_call" | custom-call | tf_op jit(solution)/shard_map/section_backward/pallas_call | solution.py:488
  70.4 0.6 copy.15
  71.0 0.6 copy.16
  71.7 0.8 %copy.17 = bf16[1,256,1024]{2,1,0:T(8,128)(2,1)} copy(bf16[1,256,1024]{2,1,0:T(8,128)(2,1)S(1)} %bitcast.11) | data formatting | bytes 1048576
  72.5 0.8 %copy.18 = bf16[1,256,1024]{2,1,0:T(8,128)(2,1)} copy(bf16[1,256,1024]{2,1,0:T(8,128)(2,1)S(1)} %bitcast.10) | data formatting | bytes 1048576

commit v3 on v2

--- a/solution.py
+++ b/solution.py
@@ -412,32 +412,42 @@
     dq_copy = remote(dq_stage, dq_out, out_ss.at[8], out_rs.at[8], before_pipe)
     start(dq_copy)
 
+    spread_wait(suf_send, suf_got, p4_ss, p4_rs)
+
+    def dv_copy(h):
+        cols = head128(h)
+        return remote(dv_stage.at[:, cols], dv_out.at[:, cols], out_ss.at[h], out_rs.at[h], before_pipe)
+
+    def suffix(h):
+        return split(jnp.concatenate([suf_got[2 * h], suf_got[2 * h + 1]], axis=0))
+
+    def value_out(h, carry):
+        cols = head128(h)
+        s_hi, s_lo = suffix(h)
+        dv = (
+            dv_acc[:, cols]
+            + mm(kt_hi[h], s_hi) + mm(kt_hi[h], s_lo) + mm(kt_lo[h], s_hi)
+        )
+        dv_stage[:, cols] = dv.astype(bf16)
+        return carry
+
+    by_groups(value_out, 0, after=lambda i: dv_copy(i).start())
+
     gather_wait(bnorm_own, bnorm_got, bn_ss, bn_rs)
     acc = jnp.zeros((8, T), f32)
     for j in reversed(range(N)):
         acc = jnp.where(j > me, bnorm_got[j] + keep[j] * acc, acc)
     bnorm_col[...] = jnp.transpose(jnp.concatenate([acc, jnp.zeros((120, T), f32)], axis=0))
-    spread_wait(suf_send, suf_got, p4_ss, p4_rs)
-
-    def dv_copy(h):
-        cols = head128(h)
-        return remote(dv_stage.at[:, cols], dv_out.at[:, cols], out_ss.at[h], out_rs.at[h], before_pipe)
-
-    def key_value_grad(h, carry):
-        cols = head128(h)
-        s_hi, s_lo = split(jnp.concatenate([suf_got[2 * h], suf_got[2 * h + 1]], axis=0))
-        dv = (
-            dv_acc[:, cols]
-            + mm(kt_hi[h], s_hi) + mm(kt_hi[h], s_lo) + mm(kt_lo[h], s_hi)
-        )
-        dv_stage[:, cols] = dv.astype(bf16)
-        v = v_in[:, cols]
+
+    def key_out(h, carry):
+        s_hi, s_lo = suffix(h)
+        v = v_in[:, head128(h)]
         col = jnp.sum(jnp.where(lane128 == h, bnorm_col[:E], 0.0), axis=1, keepdims=True)
         g = mm_nt(s_hi, v) + mm_nt(s_lo, v) + col
         dk_t[head16(h), :] += after_row * features_back(g, k_t[head16(h), :], 2.0)
         return carry
 
-    by_groups(key_value_grad, 0, after=lambda i: dv_copy(i).start())
+    by_groups(key_out, 0)
     dk_stage[...] = (jnp.transpose(dk_t[...]) * 0.5).astype(bf16)
     dk_copy = remote(dk_stage, dk_out, out_ss.at[10], out_rs.at[10], before_pipe)
     start(dk_copy)

time: 73.4 us -> 73.4 us (level)
  no operation moved by 1% of the time
where the time goes in v3:
time: 73.4 us; the launch traced here: 73.2 us
  Pallas kernels  69.8 us (95%)
  local copies, waits for them, and re-layouts  2.85 us (4%)
    pallas_call x1, Pallas kernels, on_device(): pl.pallas_call(body, out_shape=tuple((pltpu.VMEM(x, bf16) for x in shapes...  69.8 us
    unnamed x4, local copies, waits for them, and re-layouts  2.85 us

profile of v3, /device:TPU:6, one launch (start us, length us, event | category | flops | bytes accessed | tf_op | source)
XLA Modules:
  0.0 73.2 jit_solution(6952025243879283974)
XLA Ops:
  0.6 69.8 %section_backward.1 = (bf16[256,128]{1,0:T(8,128)(2,1)S(1)}, bf16[256,128]{1,0:T(8,128)(2,1)S(1)}, bf16[256,1024]{1,0:T(8,128)(2,1)S(1)}, bf16[256,1024]{1,0:T(8,128)(2,1)S(1)}) custom-call(s32[1,16]{1,0:T(1,128)} %bounds.1, bf16[256,128]{1,0:T(8,128)(2,1)} %bitcast.17, bf16[256,128]{1,0:T(8,128)(2,1)} %bitcast.18, bf16[256,1024]{1,0:T(8,128)(2,1)} %bitcast.14, ...), custom_call_target="tpu_custom_call" | custom-call | tf_op jit(solution)/shard_map/section_backward/pallas_call | solution.py:498
  70.4 0.6 copy.15
  71.0 0.6 copy.16
  71.7 0.8 %copy.17 = bf16[1,256,1024]{2,1,0:T(8,128)(2,1)} copy(bf16[1,256,1024]{2,1,0:T(8,128)(2,1)S(1)} %bitcast.11) | data formatting | bytes 1048576
  72.5 0.8 %copy.18 = bf16[1,256,1024]{2,1,0:T(8,128)(2,1)} copy(bf16[1,256,1024]{2,1,0:T(8,128)(2,1)S(1)} %bitcast.10) | data formatting | bytes 1048576
